TPU v7x, 32 devices: a whole 2x2x4 slice. The times are simulated.
32 devices in a mesh: face: 4 (over x, core), tile: 8 (over z, y).
Axes of the slice: x: 2, y: 2, z: 4, core: 2. Of those that a mesh axis runs over, the one named last changes fastest.
Arguments:
- field_in: bfloat16 [12, 48, 256, 256], P('face', None, 'tile'), may hold values from -6 to 6
- out_grad: bfloat16 [12, 48, 256, 256], P('face', None, 'tile'), may hold values from -6 to 6
- weight_first: bfloat16 [48, 48, 3, 3], replicated, may hold values from -0.3125 to 0.3125
- bias_first: float32 [48], replicated, may hold values from -3 to 3
- weight_second: bfloat16 [48, 48, 3, 3], replicated, may hold values from -0.3125 to 0.3125
- bias_second: float32 [48], replicated, may hold values from -3 to 3
- face_links: int32 [12, 4, 3], replicated, may hold values from 0 to 11, as said below
- corner_rules: int32 [12, 4], replicated, may hold values from 0 to 1
Outputs:
- output_field: bfloat16 [12, 48, 256, 256], P('face', None, 'tile')
- grad_field: bfloat16 [12, 48, 256, 256], P('face', None, 'tile')
- grad_weight_first: float32 [48, 48, 3, 3], replicated
- grad_bias_first: float32 [48], replicated
- grad_weight_second: float32 [48, 48, 3, 3], replicated
- grad_bias_second: float32 [48], replicated
Inputs may be any that keep to these rules, and one draw needn't show every extreme that they name: face_links[f, e] = (g, e2, r) glues edge e of face f to edge e2 of face g; r = 1 when positions along the two edges run in opposite directions. The gluing is a pairing: (g, e2) differs from (f, e) and face_links[g, e2] = (f, e, r). The partner face lies in 0..11, the edge in 0..3, the flag in 0..1.
All inputs are finite; a program needn't handle non-finite values.
Results may differ from a plain program's by a relative error of at most 0.0055.
The roundings to bfloat16 on the way count: a program that leaves them out, or rounds other values in their place, can miss the bound.
Values may be sent and summed in bfloat16 or wider, within the bound.
A program may use at most 256 MiB of HBM per device.

v0:
```python
import jax
import jax.numpy as jnp
from jax import lax
from jax.sharding import PartitionSpec as P

INV_ROOT_TWO = 0.7071067811865476
INV_ROOT_TWO_PI = 0.3989422804014327


def shortened(x):
    return jax.tree.map(lambda a: a.astype(jnp.bfloat16) if a.dtype == jnp.float32 else a, x)


def extended_2(block, sides, width):
    for axis, dim in sides:
        count = lax.axis_size(axis)
        forward = [(i, i + 1) for i in range(count - 1)]
        backward = [(target, source) for source, target in forward]
        low = lax.ppermute(
            lax.slice_in_dim(block, block.shape[dim] - width, None, axis=dim), axis, forward
        )
        high = lax.ppermute(lax.slice_in_dim(block, 0, width, axis=dim), axis, backward)
        block = jnp.concatenate([low, block, high], axis=dim)
    return block


def gelu_pair(values):
    normal_cdf = 0.5 * (1.0 + lax.erf(values * INV_ROOT_TWO))
    normal_pdf = jnp.exp(-0.5 * values * values) * INV_ROOT_TWO_PI
    return (values * normal_cdf, normal_cdf + values * normal_pdf)


def convolve(padded, weight):
    return lax.conv_general_dilated(
        padded,
        weight,
        (1, 1),
        "VALID",
        dimension_numbers=("NCHW", "OIHW", "NCHW"),
        preferred_element_type=jnp.float32,
    )


def halo_rows(strip):
    return extended_2(shortened(strip), (("tile", 2),), 1).astype(strip.dtype)


def place_lines(north_row, south_row, west_part, east_part, tile_pos, tile_count):
    seg_len = west_part.shape[-1]
    mirrored = tile_count - 1 - tile_pos
    blanks = jnp.zeros(north_row.shape, jnp.float32)
    north_full = jnp.where(tile_pos == 0, north_row.astype(jnp.float32), blanks)
    south_full = jnp.where(tile_pos == tile_count - 1, south_row.astype(jnp.float32), blanks)
    west_wide = west_part.astype(jnp.float32)
    east_wide = east_part.astype(jnp.float32)
    west_full = lax.dynamic_update_slice_in_dim(blanks, west_wide, tile_pos * seg_len, 2)
    east_full = lax.dynamic_update_slice_in_dim(blanks, east_wide, tile_pos * seg_len, 2)
    placed = jnp.stack([north_full, south_full, west_full, east_full], axis=1)
    own_lines = lax.psum(placed.astype(jnp.bfloat16), "tile")
    front = lax.dynamic_slice_in_dim(own_lines, tile_pos * seg_len, seg_len, 3)
    back = lax.dynamic_slice_in_dim(own_lines, mirrored * seg_len, seg_len, 3)
    return (front, back)


def partner_pieces(front, my_links, tile_pos, tile_count):
    faces_dev, _, channels, seg_len = front.shape
    side_len = seg_len * tile_count
    partner_face = my_links[:, :, 0].reshape(-1)
    partner_edge = my_links[:, :, 1].reshape(-1)
    flip_mask = (my_links[:, :, 2] == 1).reshape(-1)
    gathered = lax.all_gather(front, ("face", "tile"), axis=3, tiled=True)

    def fetch_line(face_id, edge_id):
        start = (face_id % faces_dev, edge_id, 0, face_id // faces_dev * side_len)
        return lax.dynamic_slice(gathered, start, (1, 1, channels, side_len))[0, 0]

    source = jax.vmap(fetch_line)(partner_face, partner_edge)
    ghosts = jnp.where(flip_mask[:, None, None], source[:, :, ::-1], source)
    ghosts = ghosts.reshape(faces_dev, 4, channels, side_len)
    north_row = ghosts[:, 0]
    south_row = ghosts[:, 1]
    west_part = lax.dynamic_slice_in_dim(ghosts[:, 2], tile_pos * seg_len, seg_len, 2)
    east_part = lax.dynamic_slice_in_dim(ghosts[:, 3], tile_pos * seg_len, seg_len, 2)
    return (north_row, south_row, west_part, east_part)


def fill_strip(activation, my_links, my_corners, tile_pos, tile_count):
    front, back = place_lines(
        activation[:, :, 0, :],
        activation[:, :, -1, :],
        activation[:, :, :, 0],
        activation[:, :, :, -1],
        tile_pos,
        tile_count,
    )
    north_row, south_row, west_part, east_part = partner_pieces(
        front, my_links, tile_pos, tile_count
    )
    corner_code = (my_corners == 0)[:, :, None]
    corner_nw = jnp.where(corner_code[:, 0], north_row[:, :, 0], west_part[:, :, 0])
    corner_ne = jnp.where(corner_code[:, 1], north_row[:, :, -1], east_part[:, :, 0])
    corner_sw = jnp.where(corner_code[:, 2], south_row[:, :, 0], west_part[:, :, -1])
    corner_se = jnp.where(corner_code[:, 3], south_row[:, :, -1], east_part[:, :, -1])
    middle = jnp.concatenate(
        [west_part[:, :, :, None], activation, east_part[:, :, :, None]], axis=3
    )
    extended = halo_rows(middle)
    top_row = jnp.concatenate([corner_nw[:, :, None], north_row, corner_ne[:, :, None]], axis=2)
    bottom_row = jnp.concatenate([corner_sw[:, :, None], south_row, corner_se[:, :, None]], axis=2)
    top_rim = jnp.where(tile_pos == 0, top_row, extended[:, :, 0])
    bottom_rim = jnp.where(tile_pos == tile_count - 1, bottom_row, extended[:, :, -1])
    return jnp.concatenate(
        [top_rim[:, :, None], extended[:, :, 1:-1], bottom_rim[:, :, None]], axis=2
    )


def unfold_strip(cotangent, weight, my_links, my_corners, tile_pos, tile_count):
    widened = jnp.pad(cotangent, ((0, 0), (0, 0), (0, 0), (1, 1)))
    extended = halo_rows(widened)
    padded = jnp.pad(extended, ((0, 0), (0, 0), (1, 1), (1, 1)))
    flipped = jnp.transpose(weight[:, :, ::-1, ::-1], (1, 0, 2, 3))
    pad_grad = convolve(padded, flipped)
    at_top = tile_pos == 0
    at_bottom = tile_pos == tile_count - 1
    north_row = pad_grad[:, :, 0, 1:-1]
    south_row = pad_grad[:, :, -1, 1:-1]
    west_part = pad_grad[:, :, 1:-1, 0]
    east_part = pad_grad[:, :, 1:-1, -1]
    corner_nw = pad_grad[:, :, 0, 0]
    corner_ne = pad_grad[:, :, 0, -1]
    corner_sw = pad_grad[:, :, -1, 0]
    corner_se = pad_grad[:, :, -1, -1]
    corner_code = my_corners[:, :, None]
    north_row = north_row.at[:, :, 0].add(jnp.where(corner_code[:, 0] == 0, corner_nw, 0.0))
    north_row = north_row.at[:, :, -1].add(jnp.where(corner_code[:, 1] == 0, corner_ne, 0.0))
    south_row = south_row.at[:, :, 0].add(jnp.where(corner_code[:, 2] == 0, corner_sw, 0.0))
    south_row = south_row.at[:, :, -1].add(jnp.where(corner_code[:, 3] == 0, corner_se, 0.0))
    west_part = west_part.at[:, :, 0].add(
        jnp.where((corner_code[:, 0] == 1) & at_top, corner_nw, 0.0)
    )
    west_part = west_part.at[:, :, -1].add(
        jnp.where((corner_code[:, 2] == 1) & at_bottom, corner_sw, 0.0)
    )
    east_part = east_part.at[:, :, 0].add(
        jnp.where((corner_code[:, 1] == 1) & at_top, corner_ne, 0.0)
    )
    east_part = east_part.at[:, :, -1].add(
        jnp.where((corner_code[:, 3] == 1) & at_bottom, corner_se, 0.0)
    )
    front, back = place_lines(
        north_row.astype(jnp.bfloat16),
        south_row.astype(jnp.bfloat16),
        west_part.astype(jnp.bfloat16),
        east_part.astype(jnp.bfloat16),
        tile_pos,
        tile_count,
    )
    back_north, back_south, back_west, back_east = partner_pieces(
        front, my_links, tile_pos, tile_count
    )
    interior = pad_grad[:, :, 1:-1, 1:-1]
    interior = interior.at[:, :, 0, :].add(jnp.where(at_top, back_north.astype(jnp.float32), 0.0))
    interior = interior.at[:, :, -1, :].add(
        jnp.where(at_bottom, back_south.astype(jnp.float32), 0.0)
    )
    interior = interior.at[:, :, :, 0].add(back_west.astype(jnp.float32))
    interior = interior.at[:, :, :, -1].add(back_east.astype(jnp.float32))
    return interior


def weight_grad(cotangent, padded):
    return lax.conv_general_dilated(
        padded,
        cotangent,
        (1, 1),
        "VALID",
        dimension_numbers=("CNHW", "IOHW", "CNHW"),
        preferred_element_type=jnp.float32,
    )


def body(
    field_in,
    out_grad,
    weight_first,
    bias_first,
    weight_second,
    bias_second,
    face_links,
    corner_rules,
):
    tile_count = lax.axis_size("tile")
    tile_pos = lax.axis_index("tile")
    face_pos = lax.axis_index("face")
    faces_dev = field_in.shape[0]
    side_len = field_in.shape[3]
    my_links = lax.dynamic_slice_in_dim(face_links, face_pos * faces_dev, faces_dev, 0)
    my_corners = lax.dynamic_slice_in_dim(corner_rules, face_pos * faces_dev, faces_dev, 0)
    padded_first = fill_strip(field_in, my_links, my_corners, tile_pos, tile_count)
    pre_first = convolve(padded_first, weight_first) + bias_first[None, :, None, None]
    gelu_first, slope_first = gelu_pair(pre_first)
    hidden = gelu_first.astype(jnp.bfloat16)
    padded_second = fill_strip(hidden, my_links, my_corners, tile_pos, tile_count)
    pre_second = convolve(padded_second, weight_second) + bias_second[None, :, None, None]
    gelu_second, slope_second = gelu_pair(pre_second)
    output_field = gelu_second.astype(jnp.bfloat16)
    grad_second = (out_grad.astype(jnp.float32) * slope_second).astype(jnp.bfloat16)
    weight_second_part = weight_grad(grad_second, padded_second)
    bias_second_part = jnp.sum(grad_second.astype(jnp.float32), axis=(0, 2, 3))
    grad_hidden = unfold_strip(
        grad_second, weight_second, my_links, my_corners, tile_pos, tile_count
    )
    grad_first = (grad_hidden * slope_first).astype(jnp.bfloat16)
    weight_first_part = weight_grad(grad_first, padded_first)
    bias_first_part = jnp.sum(grad_first.astype(jnp.float32), axis=(0, 2, 3))
    grad_field = unfold_strip(
        grad_first, weight_first, my_links, my_corners, tile_pos, tile_count
    ).astype(jnp.bfloat16)
    totals = lax.psum(
        (weight_first_part, bias_first_part, weight_second_part, bias_second_part), ("face", "tile")
    )
    return (
        output_field,
        grad_field,
        totals[0] / side_len,
        totals[1] / side_len,
        totals[2] / side_len,
        totals[3] / side_len,
    )


def solution(mesh):
    return jax.shard_map(
        body,
        mesh=mesh,
        in_specs=(
            P("face", None, "tile", None),
            P("face", None, "tile", None),
            P(),
            P(),
            P(),
            P(),
            P(),
            P(),
        ),
        out_specs=(
            P("face", None, "tile", None),
            P("face", None, "tile", None),
            P(),
            P(),
            P(),
            P(),
        ),
        check_vma=False,
    )
```

profile of v0, /device:TPU:0, one launch (start us, length us, event | category | flops | bytes accessed | tf_op | source)
XLA Modules:
  0.0 1963.4 jit_solution(1567796698921269111)
XLA Ops:
  19.2 74.5 %all-reduce.10.cloned.1.call-done = bf16[3,4,48,256]{3,2,0,1:T(8,128)(2,1)} async-done(((bf16[3,4,48,256]{3,2,0,1:T(8,128)(2,1)}), bf16[3,4,48,256]{3,2,0,1:T(8,128)(2,1)}) %all-reduce.10.cloned.1.call-update) | async-done | bytes 294928 | tf_op jit(solution)/shard_map/psum | solution.py:59
  103.9 51.9 %all-gather.5.cloned.1.call-done = bf16[3,4,48,1024]{2,1,0,3:T(4,128)(2,1)} async-done(((bf16[3,4,48,32]{2,1,0,3:T(4,128)(2,1)}), bf16[3,4,48,1024]{2,1,0,3:T(4,128)(2,1)}) %all-gather.5.cloned.1.call-update) | async-done | bytes 1179664 | tf_op jit(solution)/shard_map/all_gather | solution.py:71
  179.5 17.8 fusion.87
  203.9 24.2 %copy.2867 = bf16[48,34,3,8,33]{4,3,0,2,1:T(8,128)(2,1)} copy(bf16[48,34,3,8,33]{0,2,4,3,1:T(4,128)(2,1)} %bitcast.324) | data formatting | bytes 5170176 | tf_op jit(solution)/shard_map/conv_general_dilated | solution.py:34
  228.1 11.7 slice.977
  239.8 15.0 fusion.13
  254.8 14.0 copy.2762
  268.8 23.4 %fusion.8 = (f32[32,24,33,48]{3,1,2,0:T(8,128)}, bf16[32,24,33,48]{3,1,2,0:T(8,128)(2,1)S(1)}) fusion(f32[48]{0:T(128)S(1)} %copy-done.49, pred[24,33]{0,1:T(8,128)(4,1)S(1)} %copy-done.53, bf16[48,48,3,3]{1,0,3,2:T(8,128)(2,1)S(1)} %copy-done.47, bf16[48,34,3,8,35]{0,3,2,4,1:T(8,128)(2,1)} %copy.2762), kind=kOutput, calls=%fused_computation.21 | convolution fusion | flops 1065664512 | bytes 10083288 | tf_op jit(solution)/shard_map/conv_general_dilated | solution.py:34
  311.7 72.1 %all-reduce.12.cloned.1.call-done = bf16[3,4,48,256]{3,2,0,1:T(8,128)(2,1)} async-done(((bf16[3,4,48,256]{3,2,0,1:T(8,128)(2,1)}), bf16[3,4,48,256]{3,2,0,1:T(8,128)(2,1)}) %all-reduce.12.cloned.1.call-update) | async-done | bytes 294928 | tf_op jit(solution)/shard_map/psum | solution.py:59
  386.0 59.4 %all-gather.7.cloned.1.call-done = bf16[3,4,48,1024]{2,1,0,3:T(4,128)(2,1)} async-done(((bf16[3,4,48,32]{2,1,0,3:T(4,128)(2,1)}), bf16[3,4,48,1024]{2,1,0,3:T(4,128)(2,1)}) %all-gather.7.cloned.1.call-update) | async-done | bytes 1179664 | tf_op jit(solution)/shard_map/all_gather | solution.py:71
  468.6 19.1 fusion.84
  494.3 24.2 %copy.2872 = bf16[48,34,3,8,33]{4,3,0,2,1:T(8,128)(2,1)} copy(bf16[48,34,3,8,33]{0,2,4,3,1:T(4,128)(2,1)} %bitcast.325) | data formatting | bytes 5170176 | tf_op jit(solution)/shard_map/conv_general_dilated | solution.py:34
  530.2 15.0 fusion.14
  545.2 14.0 copy.2782
  559.2 22.5 %fusion.12 = (f32[32,24,33,48]{3,1,2,0:T(8,128)}, bf16[32,24,33,48]{3,1,2,0:T(8,128)(2,1)}) fusion(f32[48]{0:T(128)S(1)} %copy-done.50, pred[24,33]{0,1:T(8,128)(4,1)S(1)} %copy-done.53, bf16[48,48,3,3]{1,0,3,2:T(8,128)(2,1)S(1)} %copy-done, bf16[48,34,3,8,35]{0,3,2,4,1:T(8,128)(2,1)} %copy.2782), kind=kOutput, calls=%fused_computation.25 | convolution fusion | flops 1065664512 | bytes 10083288 | tf_op jit(solution)/shard_map/conv_general_dilated | solution.py:34
  581.7 11.9 copy.2784
  639.9 14.1 reshape.1719
  665.8 15.0 fusion.15
  680.7 14.0 copy.2790
  694.7 22.0 %convolution_select_fusion.1 = f32[34,24,33,48]{3,1,2,0:T(8,128)} fusion(bf16[48,48,3,3]{1,0,3,2:T(8,128)(2,1)S(1)} %copy-done, bf16[48,34,3,8,35]{0,3,2,4,1:T(8,128)(2,1)} %copy.2790, pred[24,33]{0,1:T(8,128)(4,1)S(1)} %copy-done.51), kind=kOutput, calls=%fused_computation.37 | convolution fusion | flops 1096153344 | bytes 7954200 | tf_op jit(solution)/shard_map/conv_general_dilated | solution.py:34
  716.7 13.6 copy.2791
  730.3 15.7 reshape.1723
  746.0 17.6 copy.2888
  763.6 29.2 %fusion.67 = (f32[3,48,1,256]{2,1,0,3:T(8,128)}, f32[3,48,1,256]{2,1,0,3:T(8,128)}) fusion(f32[3,48,34,258]{2,1,0,3:T(8,128)} %bitcast.309), kind=kLoop, calls=%fused_computation.219 | loop fusion | bytes 589824 | tf_op jit(solution)/shard_map/slice | solution.py:125
  793.9 13.2 copy.2798
  807.1 13.2 copy.2793
  827.4 73.5 %all-reduce.14.cloned.1.call-done = bf16[3,4,48,256]{3,2,0,1:T(8,128)(2,1)} async-done(((bf16[3,4,48,256]{3,2,0,1:T(8,128)(2,1)}), bf16[3,4,48,256]{3,2,0,1:T(8,128)(2,1)}) %all-reduce.14.cloned.1.call-update) | async-done | bytes 294928 | tf_op jit(solution)/shard_map/psum | solution.py:59
  902.8 11.8 copy.2822
  925.3 16.4 copy.2891
  948.4 16.5 slice.1002
  970.2 12.2 copy.2815
  982.4 20.5 %slice_add_fusion.3 = f32[3,48,1,256]{2,1,0,3:T(8,128)} fusion(f32[3,48,1,256]{2,1,0,3:T(8,128)} %copy.2815, f32[3,48,34,258]{2,1,0,3:T(8,128)} %bitcast.315), kind=kLoop, calls=%fused_computation.14 | loop fusion | flops 36864 | bytes 442368 | tf_op jit(solution)/shard_map/add | solution.py:162
  1003.0 12.2 copy.2817
  1015.1 43.6 %scatter-add.94 = f32[3,48,32,256]{2,1,0,3:T(8,128)} dynamic-update-slice(f32[3,48,32,256]{2,1,0,3:T(8,128)} %slice.1002, f32[3,48,1,256]{2,1,0,3:T(8,128)} %slice_add_fusion.3, s32[]{:T(128)} %constant.616.clone.1, s32[]{:T(128)} %constant.616.clone.1, s32[]{:T(128)} %constant.616.clone.1, s32[]{:T(128)} %constant.616.clone.1) | dynamic-update-slice | bytes 294916 | tf_op jit(solution)/shard_map/scatter-add | solution.py:162
  1058.7 20.5 %slice_add_fusion.2 = f32[3,48,1,256]{2,1,0,3:T(8,128)} fusion(f32[3,48,1,256]{2,1,0,3:T(8,128)} %copy.2817, f32[3,48,32,256]{2,1,0,3:T(8,128)} %scatter-add.94), kind=kLoop, calls=%fused_computation.13 | loop fusion | flops 36864 | bytes 442368 | tf_op jit(solution)/shard_map/add | solution.py:163
  1079.2 73.5 %scatter-add.95 = f32[3,48,32,256]{2,1,0,3:T(8,128)} dynamic-update-slice(f32[3,48,32,256]{2,1,0,3:T(8,128)} %scatter-add.94, f32[3,48,1,256]{2,1,0,3:T(8,128)} %slice_add_fusion.2, s32[]{:T(128)} %constant.616.clone.1, s32[]{:T(128)} %constant.616.clone.1, s32[]{:T(128)} %constant.635.clone.1, s32[]{:T(128)} %constant.616.clone.1) | dynamic-update-slice | bytes 294916 | tf_op jit(solution)/shard_map/scatter-add | solution.py:163
  1155.9 13.3 convert_reduce_fusion
  1179.1 12.1 copy.2824
  1207.4 44.8 %fusion.75 = f32[48,48,3,3]{0,1,3,2:T(8,128)} fusion(bf16[3,48,32,256]{1,0,3,2:T(4,128)(2,1)} %copy.2858, bf16[3,48,1,258]{1,0,3,2:T(4,128)(2,1)S(1)} %copy-done.15, bf16[3,48,32,1]{1,0,3,2:T(4,128)(2,1)S(1)} %copy-done.23, bf16[3,48,32,256]{1,0,3,2:T(4,128)(2,1)} %bitcast.319, bf16[3,48,32,1]{1,0,3,2:T(4,128)(2,1)S(1)} %copy-done.21, ...), kind=kOutput, calls=%fused_computation.227 | convolution fusion | flops 1031847552 | bytes 4968576 | tf_op jit(solution)/shard_map/conv_general_dilated | solution.py:172
  1252.2 15.0 copy.2857
  1267.3 12.5 copy.2905
  1287.3 14.3 reshape.1726
  1301.6 11.7 slice.1028
  1313.3 15.0 fusion.16
  1328.2 14.0 copy.2828
  1342.3 21.8 %convolution_select_fusion = f32[34,24,33,48]{3,1,2,0:T(8,128)} fusion(bf16[48,48,3,3]{1,0,3,2:T(8,128)(2,1)S(1)} %copy-done.48, bf16[48,34,3,8,35]{0,3,2,4,1:T(8,128)(2,1)} %copy.2828, pred[24,33]{0,1:T(8,128)(4,1)S(1)} %copy-done.52), kind=kOutput, calls=%fused_computation.36 | convolution fusion | flops 1096153344 | bytes 7954200 | tf_op jit(solution)/shard_map/conv_general_dilated | solution.py:34
  1364.1 13.6 copy.2829
  1377.7 15.7 reshape.1730
  1393.4 17.6 copy.2892
  1411.0 29.3 %fusion.66 = (f32[3,48,1,256]{2,1,0,3:T(8,128)}, f32[3,48,1,256]{2,1,0,3:T(8,128)}) fusion(f32[3,48,34,258]{2,1,0,3:T(8,128)} %bitcast.302), kind=kLoop, calls=%fused_computation.218 | loop fusion | bytes 589824 | tf_op jit(solution)/shard_map/slice | solution.py:125
  1442.5 13.2 copy.2835
  1455.8 13.3 copy.2831
  1475.0 44.8 %fusion.74 = f32[48,48,3,3]{0,1,3,2:T(8,128)} fusion(bf16[3,48,32,256]{1,0,3,2:T(4,128)(2,1)} %copy.2857, bf16[3,48,1,258]{1,0,3,2:T(4,128)(2,1)S(1)} %copy-done.11, bf16[3,48,32,1]{1,0,3,2:T(4,128)(2,1)S(1)} %copy-done.19, bf16[3,48,32,256]{1,0,3,2:T(4,128)(2,1)} %copy.2758, bf16[3,48,32,1]{1,0,3,2:T(4,128)(2,1)S(1)} %copy-done.17, ...), kind=kOutput, calls=%fused_computation.226 | convolution fusion | flops 1031847552 | bytes 4968576 | tf_op jit(solution)/shard_map/conv_general_dilated | solution.py:172
  1520.1 28.0 %all-reduce.16.cloned.1.call-done = bf16[3,4,48,256]{3,2,0,1:T(8,128)(2,1)} async-done(((bf16[3,4,48,256]{3,2,0,1:T(8,128)(2,1)}), bf16[3,4,48,256]{3,2,0,1:T(8,128)(2,1)}) %all-reduce.16.cloned.1.call-update) | async-done | bytes 294928 | tf_op jit(solution)/shard_map/psum | solution.py:59
  1567.8 39.3 %all-reduce.2 = (f32[48]{0:T(128)S(1)}, f32[48]{0:T(128)S(1)}) all-reduce(f32[48]{0:T(128)S(1)} %copy-done.46, f32[48]{0:T(128)S(1)} %copy-done.45), channel_id=1, replica_groups=mesh['face'=4,'tile'=8] {'face','tile'}, use_global_device_ids=true, to_apply=%region_6.7 | all-reduce | flops 96 | bytes 768 | tf_op jit(solution)/shard_map/psum | solution.py:219
  1608.2 16.6 slice.1030
  1624.8 54.6 %all-reduce.18.cloned.1.call-done = (f32[48,48,3,3]{0,1,3,2:T(8,128)}, f32[48,48,3,3]{0,1,3,2:T(8,128)}) async-done(((f32[48,48,3,3]{0,1,3,2:T(8,128)}, f32[48,48,3,3]{0,1,3,2:T(8,128)}), (f32[48,48,3,3]{0,1,3,2:T(8,128)}, f32[48,48,3,3]{0,1,3,2:T(8,128)})) %all-reduce.18.cloned.1.call-update) | async-done | bytes 165904 | tf_op jit(solution)/shard_map/psum | solution.py:219
  1683.0 60.5 %all-gather.11.cloned.1.call-done = bf16[3,4,48,1024]{2,1,0,3:T(4,128)(2,1)} async-done(((bf16[3,4,48,32]{2,1,0,3:T(4,128)(2,1)}), bf16[3,4,48,1024]{2,1,0,3:T(4,128)(2,1)}) %all-gather.11.cloned.1.call-update) | async-done | bytes 1179664 | tf_op jit(solution)/shard_map/all_gather | solution.py:71
  1748.4 12.2 copy.2852
  1760.5 20.5 %slice_add_fusion.1 = f32[3,48,1,256]{2,1,0,3:T(8,128)} fusion(f32[3,48,1,256]{2,1,0,3:T(8,128)} %copy.2852, f32[3,48,34,258]{2,1,0,3:T(8,128)} %bitcast.308), kind=kLoop, calls=%fused_computation.12 | loop fusion | flops 36864 | bytes 442368 | tf_op jit(solution)/shard_map/add | solution.py:162
  1781.0 12.2 copy.2854
  1793.2 43.6 %scatter-add.114 = f32[3,48,32,256]{2,1,0,3:T(8,128)} dynamic-update-slice(f32[3,48,32,256]{2,1,0,3:T(8,128)} %slice.1030, f32[3,48,1,256]{2,1,0,3:T(8,128)} %slice_add_fusion.1, s32[]{:T(128)} %constant.616.clone.1, s32[]{:T(128)} %constant.616.clone.1, s32[]{:T(128)} %constant.616.clone.1, s32[]{:T(128)} %constant.616.clone.1) | dynamic-update-slice | bytes 294916 | tf_op jit(solution)/shard_map/scatter-add | solution.py:162
  1836.8 20.5 %slice_add_fusion = f32[3,48,1,256]{2,1,0,3:T(8,128)} fusion(f32[3,48,1,256]{2,1,0,3:T(8,128)} %copy.2854, f32[3,48,32,256]{2,1,0,3:T(8,128)} %scatter-add.114), kind=kLoop, calls=%fused_computation.11 | loop fusion | flops 36864 | bytes 442368 | tf_op jit(solution)/shard_map/add | solution.py:163
  1857.3 73.6 %scatter-add.115 = f32[3,48,32,256]{2,1,0,3:T(8,128)} dynamic-update-slice(f32[3,48,32,256]{2,1,0,3:T(8,128)} %scatter-add.114, f32[3,48,1,256]{2,1,0,3:T(8,128)} %slice_add_fusion, s32[]{:T(128)} %constant.616.clone.1, s32[]{:T(128)} %constant.616.clone.1, s32[]{:T(128)} %constant.635.clone.1, s32[]{:T(128)} %constant.616.clone.1) | dynamic-update-slice | bytes 294916 | tf_op jit(solution)/shard_map/scatter-add | solution.py:163
  (333 shorter events, 305.3 us)
Async XLA Ops:
  7.2 552.0 %copy-start = (bf16[48,48,3,3]{1,0,3,2:T(8,128)(2,1)S(1)}, bf16[48,48,3,3]{1,0,3,2:T(8,128)(2,1)}, u32[]{:S(2)}) copy-start(bf16[48,48,3,3]{1,0,3,2:T(8,128)(2,1)} %param.60) | copy-start | bytes 124420
  7.2 88.4 %copy-start.4 = (bf16[3,48,32,256]{3,2,1,0:T(8,128)(2,1)S(1)}, bf16[3,48,32,256]{3,2,1,0:T(8,128)(2,1)}, u32[]{:S(2)}) copy-start(bf16[3,48,32,256]{3,2,1,0:T(8,128)(2,1)} %param.56) | copy-start | bytes 7077892
  7.2 86.5 %all-reduce.10.cloned.1.call-start = ((), (), s32[]{:S(2)}) async-start(), calls=%async_computation | async-start | bytes 589824 | tf_op jit(solution)/shard_map/psum | solution.py:59
  7.2 95.1 %copy-start.24 = (s32[12,4,3]{0,1,2:T(4,128)S(1)}, s32[12,4,3]{0,1,2:T(4,128)}, u32[]{:S(2)}) copy-start(s32[12,4,3]{0,1,2:T(4,128)} %param.62) | copy-start | bytes 1732
  7.3 96.2 %copy-start.44 = (s32[12,4]{0,1:T(4,128)S(1)}, s32[12,4]{0,1:T(4,128)}, u32[]{:S(2)}) copy-start(s32[12,4]{0,1:T(4,128)} %param.63) | copy-start | bytes 580
  19.2 136.6 %all-gather.5.cloned.1.call-start = ((), (), s32[]{:S(2)}) async-start(), calls=%async_computation.1 | async-start | bytes 3244032 | tf_op jit(solution)/shard_map/all_gather | solution.py:71
  95.5 288.3 %all-reduce.12.cloned.1.call-start = ((), (), s32[]{:S(2)}) async-start(), calls=%async_computation.2 | async-start | bytes 589824 | tf_op jit(solution)/shard_map/psum | solution.py:59
  103.4 345.7 %copy-start.25 = (pred[12]{0:T(512)(128)(4,1)}, pred[12]{0:T(512)(128)(4,1)S(1)}, u32[]{:S(2)}) copy-start(pred[12]{0:T(512)(128)(4,1)S(1)} %eq.133) | copy-start | bytes 40
  103.9 341.5 %copy-start.5 = (s32[12]{0:T(128)}, s32[12]{0:T(128)S(1)}, u32[]{:S(2)}) copy-start(s32[12]{0:T(128)S(1)} %fusion.63) | copy-start | bytes 148
  161.7 35.6 %copy-start.16 = (bf16[3,48,32,1]{1,0,3,2:T(4,128)(2,1)}, bf16[3,48,32,1]{1,0,3,2:T(4,128)(2,1)S(1)}, u32[]{:S(2)}) copy-start(bf16[3,48,32,1]{1,0,3,2:T(4,128)(2,1)S(1)} %copy.2757) | copy-start | bytes 27652
  161.8 35.5 %copy-start.18 = (bf16[3,48,32,1]{1,0,3,2:T(4,128)(2,1)}, bf16[3,48,32,1]{1,0,3,2:T(4,128)(2,1)S(1)}, u32[]{:S(2)}) copy-start(bf16[3,48,32,1]{1,0,3,2:T(4,128)(2,1)S(1)} %copy.2759) | copy-start | bytes 27652
  161.8 17.6 copy-start.3
  163.5 15.4 collective-permute-start
  167.1 12.0 collective-permute-start.1
  179.2 24.7 %copy-start.8 = (bf16[3,48,1,258]{1,0,3,2:T(4,128)(2,1)}, bf16[3,48,1,258]{1,0,3,2:T(4,128)(2,1)S(1)}, u32[]{:S(2)}) copy-start(bf16[3,48,1,258]{1,0,3,2:T(4,128)(2,1)S(1)} %maximum_select_fusion) | copy-start | bytes 222916
  179.5 24.5 %copy-start.10 = (bf16[3,48,1,258]{1,0,3,2:T(4,128)(2,1)}, bf16[3,48,1,258]{1,0,3,2:T(4,128)(2,1)S(1)}, u32[]{:S(2)}) copy-start(bf16[3,48,1,258]{1,0,3,2:T(4,128)(2,1)S(1)} %maximum_select_fusion.1) | copy-start | bytes 222916
  254.8 14.0 copy-start.47
  254.8 14.0 copy-start.49
  254.8 14.0 copy-start.53
  311.7 133.7 %all-gather.7.cloned.1.call-start = ((), (), s32[]{:S(2)}) async-start(), calls=%async_computation.3 | async-start | bytes 3244032 | tf_op jit(solution)/shard_map/all_gather | solution.py:71
  385.6 515.3 %all-reduce.14.cloned.1.call-start = ((), (), s32[]{:S(2)}) async-start(), calls=%async_computation.4 | async-start | bytes 589824 | tf_op jit(solution)/shard_map/psum | solution.py:59
  451.3 36.4 %copy-start.20 = (bf16[3,48,32,1]{1,0,3,2:T(4,128)(2,1)}, bf16[3,48,32,1]{1,0,3,2:T(4,128)(2,1)S(1)}, u32[]{:S(2)}) copy-start(bf16[3,48,32,1]{1,0,3,2:T(4,128)(2,1)S(1)} %copy.2778) | copy-start | bytes 27652
  451.4 36.3 %copy-start.22 = (bf16[3,48,32,1]{1,0,3,2:T(4,128)(2,1)}, bf16[3,48,32,1]{1,0,3,2:T(4,128)(2,1)S(1)}, u32[]{:S(2)}) copy-start(bf16[3,48,32,1]{1,0,3,2:T(4,128)(2,1)S(1)} %copy.2779) | copy-start | bytes 27652
  452.9 15.1 collective-permute-start.2
  456.3 12.0 collective-permute-start.3
  468.3 26.1 %copy-start.12 = (bf16[3,48,1,258]{1,0,3,2:T(4,128)(2,1)}, bf16[3,48,1,258]{1,0,3,2:T(4,128)(2,1)S(1)}, u32[]{:S(2)}) copy-start(bf16[3,48,1,258]{1,0,3,2:T(4,128)(2,1)S(1)} %maximum_select_fusion.2) | copy-start | bytes 222916
  468.5 25.8 %copy-start.14 = (bf16[3,48,1,258]{1,0,3,2:T(4,128)(2,1)}, bf16[3,48,1,258]{1,0,3,2:T(4,128)(2,1)S(1)}, u32[]{:S(2)}) copy-start(bf16[3,48,1,258]{1,0,3,2:T(4,128)(2,1)S(1)} %maximum_select_fusion.3) | copy-start | bytes 222916
  545.2 14.0 copy-start.50
  621.4 13.5 collective-permute-start.4
  625.8 9.1 collective-permute-start.5
  627.4 192.8 %copy-start.38 = (pred[3]{0:T(512)(128)(4,1)}, pred[3]{0:T(512)(128)(4,1)S(1)}, u32[]{:S(2)}) copy-start(pred[3]{0:T(512)(128)(4,1)S(1)} %get-tuple-element.458) | copy-start | bytes 13
  627.4 192.8 %copy-start.40 = (pred[3]{0:T(512)(128)(4,1)}, pred[3]{0:T(512)(128)(4,1)S(1)}, u32[]{:S(2)}) copy-start(pred[3]{0:T(512)(128)(4,1)S(1)} %get-tuple-element.462) | copy-start | bytes 13
  627.4 192.8 %copy-start.42 = (pred[3]{0:T(512)(128)(4,1)}, pred[3]{0:T(512)(128)(4,1)S(1)}, u32[]{:S(2)}) copy-start(pred[3]{0:T(512)(128)(4,1)S(1)} %get-tuple-element.463) | copy-start | bytes 13
  627.5 194.5 %copy-start.30 = (pred[3]{0:T(512)(128)(4,1)}, pred[3]{0:T(512)(128)(4,1)S(1)}, u32[]{:S(2)}) copy-start(pred[3]{0:T(512)(128)(4,1)S(1)} %get-tuple-element.456) | copy-start | bytes 13
  627.5 194.5 %copy-start.32 = (pred[3]{0:T(512)(128)(4,1)}, pred[3]{0:T(512)(128)(4,1)S(1)}, u32[]{:S(2)}) copy-start(pred[3]{0:T(512)(128)(4,1)S(1)} %get-tuple-element.457) | copy-start | bytes 13
  627.5 194.5 %copy-start.34 = (pred[3]{0:T(512)(128)(4,1)}, pred[3]{0:T(512)(128)(4,1)S(1)}, u32[]{:S(2)}) copy-start(pred[3]{0:T(512)(128)(4,1)S(1)} %get-tuple-element.460) | copy-start | bytes 13
  627.5 194.5 %copy-start.36 = (pred[3]{0:T(512)(128)(4,1)}, pred[3]{0:T(512)(128)(4,1)S(1)}, u32[]{:S(2)}) copy-start(pred[3]{0:T(512)(128)(4,1)S(1)} %get-tuple-element.461) | copy-start | bytes 13
  627.5 196.7 %copy-start.28 = (pred[3]{0:T(512)(128)(4,1)}, pred[3]{0:T(512)(128)(4,1)S(1)}, u32[]{:S(2)}) copy-start(pred[3]{0:T(512)(128)(4,1)S(1)} %get-tuple-element.459) | copy-start | bytes 13
  680.7 14.0 copy-start.51
  827.4 137.6 %all-gather.9.cloned.1.call-start = ((), (), s32[]{:S(2)}) async-start(), calls=%async_computation.5 | async-start | bytes 3244032 | tf_op jit(solution)/shard_map/all_gather | solution.py:71
  902.8 645.3 %all-reduce.16.cloned.1.call-start = ((), (), s32[]{:S(2)}) async-start(), calls=%async_computation.6 | async-start | bytes 589824 | tf_op jit(solution)/shard_map/psum | solution.py:59
  948.4 16.5 copy-start.6
  948.4 20.3 %copy-start.26 = (pred[12]{0:T(512)(128)(4,1)S(1)}, pred[12]{0:T(512)(128)(4,1)}, u32[]{:S(2)}) copy-start(pred[12]{0:T(512)(128)(4,1)} %copy-done.25) | copy-start | bytes 40
  1179.0 28.3 %copy-start.13 = (bf16[3,48,1,258]{1,0,3,2:T(4,128)(2,1)S(1)}, bf16[3,48,1,258]{1,0,3,2:T(4,128)(2,1)}, u32[]{:S(2)}) copy-start(bf16[3,48,1,258]{1,0,3,2:T(4,128)(2,1)} %copy-done.12) | copy-start | bytes 222916
  1179.0 28.3 %copy-start.15 = (bf16[3,48,1,258]{1,0,3,2:T(4,128)(2,1)S(1)}, bf16[3,48,1,258]{1,0,3,2:T(4,128)(2,1)}, u32[]{:S(2)}) copy-start(bf16[3,48,1,258]{1,0,3,2:T(4,128)(2,1)} %copy-done.14) | copy-start | bytes 222916
  1179.0 28.3 %copy-start.21 = (bf16[3,48,32,1]{1,0,3,2:T(4,128)(2,1)S(1)}, bf16[3,48,32,1]{1,0,3,2:T(4,128)(2,1)}, u32[]{:S(2)}) copy-start(bf16[3,48,32,1]{1,0,3,2:T(4,128)(2,1)} %copy-done.20) | copy-start | bytes 27652
  1179.1 28.3 %copy-start.23 = (bf16[3,48,32,1]{1,0,3,2:T(4,128)(2,1)S(1)}, bf16[3,48,32,1]{1,0,3,2:T(4,128)(2,1)}, u32[]{:S(2)}) copy-start(bf16[3,48,32,1]{1,0,3,2:T(4,128)(2,1)} %copy-done.22) | copy-start | bytes 27652
  1191.2 90.2 %collective-permute-start.6 = (bf16[3,48,1,258]{3,1,2,0:T(8,128)(2,1)}, bf16[3,48,1,258]{3,1,2,0:T(8,128)(2,1)}, u32[]{:S(2)}, u32[]{:S(2)}) collective-permute-start(bf16[3,48,1,258]{3,1,2,0:T(8,128)(2,1)} %copy.2824), channel_id=1, source_target_pairs={{0,1},{1,2},{2,3},{3,4},{4,5},{5,6},{6,7},{8,9},{9,10},{10,11},{11... | collective-permute-start | bytes 222920 | tf_op jit(solution)/shard_map/ppermute | solution.py:19
  1206.1 75.3 %collective-permute-start.7 = (bf16[3,48,1,258]{3,1,2,0:T(8,128)(2,1)}, bf16[3,48,1,258]{3,1,2,0:T(8,128)(2,1)}, u32[]{:S(2)}, u32[]{:S(2)}) collective-permute-start(bf16[3,48,1,258]{3,1,2,0:T(8,128)(2,1)} %copy.2825), channel_id=1, source_target_pairs={{1,0},{2,1},{3,2},{4,3},{5,4},{6,5},{7,6},{9,8},{10,9},{11,10},{12... | collective-permute-start | bytes 222920 | tf_op jit(solution)/shard_map/ppermute | solution.py:22
  1328.2 14.0 copy-start.48
  1328.2 14.0 copy-start.52
  1411.0 29.3 %copy-start.39 = (pred[3]{0:T(512)(128)(4,1)S(1)}, pred[3]{0:T(512)(128)(4,1)}, u32[]{:S(2)}) copy-start(pred[3]{0:T(512)(128)(4,1)} %copy-done.38) | copy-start | bytes 13
  1411.0 29.3 %copy-start.41 = (pred[3]{0:T(512)(128)(4,1)S(1)}, pred[3]{0:T(512)(128)(4,1)}, u32[]{:S(2)}) copy-start(pred[3]{0:T(512)(128)(4,1)} %copy-done.40) | copy-start | bytes 13
  1411.0 29.3 %copy-start.43 = (pred[3]{0:T(512)(128)(4,1)S(1)}, pred[3]{0:T(512)(128)(4,1)}, u32[]{:S(2)}) copy-start(pred[3]{0:T(512)(128)(4,1)} %copy-done.42) | copy-start | bytes 13
  1455.7 16.0 copy-start.29
  1455.7 19.2 copy-start.9
  1455.7 19.2 copy-start.11
  1455.7 19.2 copy-start.17
  1455.7 19.2 copy-start.19
  1474.9 204.5 %all-reduce.18.cloned.1.call-start = ((), (), s32[]{:S(2)}) async-start(), calls=%async_computation.8 | async-start | bytes 884736 | tf_op jit(solution)/shard_map/psum | solution.py:219
  1519.8 223.6 %all-gather.11.cloned.1.call-start = ((), (), s32[]{:S(2)}) async-start(), calls=%async_computation.7 | async-start | bytes 3244032 | tf_op jit(solution)/shard_map/all_gather | solution.py:71
  1608.2 135.2 %copy-start.7 = (s32[12]{0:T(128)S(1)}, s32[12]{0:T(128)}, u32[]{:S(2)}) copy-start(s32[12]{0:T(128)} %copy-done.5) | copy-start | bytes 148
  1608.2 139.0 %copy-start.27 = (pred[12]{0:T(512)(128)(4,1)S(1)}, pred[12]{0:T(512)(128)(4,1)}, u32[]{:S(2)}) copy-start(pred[12]{0:T(512)(128)(4,1)} %copy-done.25) | copy-start | bytes 40
  1934.0 22.6 %copy-start.1 = (bf16[48,48,3,3]{1,0,3,2:T(8,128)(2,1)S(1)}, bf16[48,48,3,3]{1,0,3,2:T(8,128)(2,1)}, u32[]{:S(2)}) copy-start(bf16[48,48,3,3]{1,0,3,2:T(8,128)(2,1)} %param.60) | copy-start | bytes 124420
  (7 other events, 93.1 us)
Sparse Core Ops, SparseCore 0:
  19.3 74.3 all-reduce.9
  97.6 58.1 all-gather.4
  311.8 71.9 all-reduce.11
  387.2 58.1 all-gather.6
  827.5 73.4 all-reduce.13
  904.7 58.1 all-gather.8
  1475.0 72.9 all-reduce.15
  1554.0 125.3 all-reduce.17
  1683.3 60.0 all-gather.10
where the time goes:
time: 1990 us; the launch traced here: 1960 us
  local copies, waits for them, and re-layouts  973 us (49%)
  waiting for transfers between devices  499 us (25%)
  other arithmetic  236 us (12%)
  matrix products  179 us (9%)
  blocking collectives  39.3 us (2%)
  starting transfers between devices  21.1 us (1%)
    psum x4, waiting for transfers between devices, place_lines(): own_lines = lax.psum(placed.astype(jnp.bfloat16), 'tile')  248 us
    conv_general_dilated x16, local copies, waits for them, and re-layouts, convolve(): lax.conv_general_dilated(padded, weight, (1, 1), 'VALID', dimension_numbe...  238 us
    all_gather x4, waiting for transfers between devices, partner_pieces(): gathered = lax.all_gather(front, ('face', 'tile'), axis=3, tiled=True)  172 us
    scatter-add x2, local copies, waits for them, and re-layouts, unfold_strip(): interior.at[:, :, -1, :]  147 us
    unnamed x128, local copies, waits for them, and re-layouts  125 us
    conv_general_dilated x4, matrix products, convolve(): lax.conv_general_dilated(padded, weight, (1, 1), 'VALID', dimension_numbe...  89.7 us
    conv_general_dilated x2, matrix products, weight_grad(): lax.conv_general_dilated(padded, cotangent, (1, 1), 'VALID', dimension_nu...  89.7 us
    scatter-add x2, local copies, waits for them, and re-layouts, unfold_strip(): interior.at[:, :, 0, :]  87.2 us
  transfers between devices with their start and end apart: 17, of which 11 were waited for; matrix products, arithmetic and copies ran while one was open for 13% of the time, Pallas kernels for 0%

commit v1 on v0

--- a/solution.py
+++ b/solution.py
@@ -56,7 +56,7 @@
     west_full = lax.dynamic_update_slice_in_dim(blanks, west_wide, tile_pos * seg_len, 2)
     east_full = lax.dynamic_update_slice_in_dim(blanks, east_wide, tile_pos * seg_len, 2)
     placed = jnp.stack([north_full, south_full, west_full, east_full], axis=1)
-    own_lines = lax.psum(placed.astype(jnp.bfloat16), "tile")
+    own_lines = jnp.sum(lax.all_gather(placed.astype(jnp.bfloat16), "tile"), axis=0)
     front = lax.dynamic_slice_in_dim(own_lines, tile_pos * seg_len, seg_len, 3)
     back = lax.dynamic_slice_in_dim(own_lines, mirrored * seg_len, seg_len, 3)
     return (front, back)

time: 1990 us -> 1360 us (0.68)
  local copies, waits for them, and re-layouts: 973 us -> 497 us
  waiting for transfers between devices: 499 us -> 421 us
  other arithmetic: 236 us -> 165 us
    psum x4 -> x0, waiting for transfers between devices: 248 us -> none  [place_lines(): own_lines = lax.psum(placed.astype(jnp.bfloat16), 'tile')]
    all_gather x0 -> x4, waiting for transfers between devices: none -> 169 us  [place_lines(): lax.all_gather(placed.astype(jnp.bfloat16), 'tile')]
    scatter-add x2 -> x4, local copies, waits for them, and re-layouts: 147 us -> 11.3 us  [the longest x2 5.64 us: unfold_strip(): interior = interior.at[:, :, :, -1].add(back_east.astype(jnp.float32))]
    scatter-add x2 -> x1, local copies, waits for them, and re-layouts: 87.2 us -> 0.77 us  [unfold_strip(): interior.at[:, :, 0, :]]
    slice x4 -> x1, local copies, waits for them, and re-layouts: 84.9 us -> 0.54 us  [unfold_strip(): north_row = pad_grad[:, :, 0, 1:-1]]
    select_n x4 -> x0, local copies, waits for them, and re-layouts: 48.8 us -> none  [the longest x2 24.4 us: unfold_strip(): jnp.where(at_top, back_north.astype(jnp.float32), 0.0)]
    add x2 -> x1, other arithmetic: 41 us -> 2.47 us  [unfold_strip(): interior.at[:, :, 0, :]]
    slice x3, local copies, waits for them, and re-layouts: 38.1 us -> 1.21 us  [the longest x1 1.19 us: unfold_strip(): west_part = pad_grad[:, :, 1:-1, 0]]
  transfers between devices with their start and end apart: 17 -> 17, of which waited for: 11 -> 12; matrix products, arithmetic and copies ran while one was open for 13% -> 15% of each run, Pallas kernels for 0% -> 0%
where the time goes in v1:
time: 1360 us; the launch traced here: 1340 us
  local copies, waits for them, and re-layouts  497 us (37%)
  waiting for transfers between devices  421 us (31%)
  matrix products  184 us (14%)
  other arithmetic  165 us (12%)
  blocking collectives  39.3 us (3%)
  starting transfers between devices  21.8 us (2%)
  between operations  15.7 us (1%)
    conv_general_dilated x17, local copies, waits for them, and re-layouts, convolve(): lax.conv_general_dilated(padded, weight, (1, 1), 'VALID', dimension_numbe...  240 us
    all_gather x4, waiting for transfers between devices, partner_pieces(): gathered = lax.all_gather(front, ('face', 'tile'), axis=3, tiled=True)  186 us
    all_gather x4, waiting for transfers between devices, place_lines(): lax.all_gather(placed.astype(jnp.bfloat16), 'tile')  169 us
    conv_general_dilated x2, matrix products, weight_grad(): lax.conv_general_dilated(padded, cotangent, (1, 1), 'VALID', dimension_nu...  94.3 us
    conv_general_dilated x4, matrix products, convolve(): lax.conv_general_dilated(padded, weight, (1, 1), 'VALID', dimension_numbe...  89.9 us
    unnamed x135, local copies, waits for them, and re-layouts  89.3 us
    conv_general_dilated x4, other arithmetic, convolve(): lax.conv_general_dilated(padded, weight, (1, 1), 'VALID', dimension_numbe...  59.8 us
    add x4, local copies, waits for them, and re-layouts, gelu_pair(): return (values * normal_cdf, normal_cdf + values * normal_pdf)  45.1 us
  transfers between devices with their start and end apart: 17, of which 12 were waited for; matrix products, arithmetic and copies ran while one was open for 15% of the time, Pallas kernels for 0%

profile of v1, /device:TPU:0, one launch (start us, length us, event | category | flops | bytes accessed | tf_op | source)
XLA Modules:
  0.0 1343.4 jit_solution(3858315737199617512)
XLA Ops:
  18.4 55.7 %all-gather.9.cloned.1.call-done = bf16[8,3,4,48,256]{4,3,2,1,0:T(8,128)(2,1)} async-done(((bf16[1,3,4,48,256]{4,3,2,1,0:T(8,128)(2,1)}), bf16[8,3,4,48,256]{4,3,2,1,0:T(8,128)(2,1)}) %all-gather.9.cloned.1.call-update) | async-done | bytes 2359312 | tf_op jit(solution)/shard_map/all_gather | solution.py:59
  77.1 6.8 copy.686
  85.5 49.8 %all-gather.11.cloned.1.call-done = bf16[3,4,48,1024]{2,1,0,3:T(4,128)(2,1)} async-done(((bf16[3,4,48,32]{2,1,0,3:T(4,128)(2,1)}), bf16[3,4,48,1024]{2,1,0,3:T(4,128)(2,1)}) %all-gather.11.cloned.1.call-update) | async-done | bytes 1179664 | tf_op jit(solution)/shard_map/all_gather | solution.py:71
  148.2 10.1 collective-permute-done
  158.8 17.8 %fusion.98 = bf16[48,34,3,258]{0,2,3,1:T(4,128)(2,1)S(1)} fusion(bf16[3,48,1,258]{1,0,3,2:T(4,128)(2,1)S(1)} %maximum_select_fusion.1, bf16[3,48,32,1]{1,0,3,2:T(4,128)(2,1)S(1)} %copy.687, bf16[3,48,32,256]{1,0,3,2:T(4,128)(2,1)S(1)} %copy-done.2, bf16[3,48,32,1]{1,0,3,2:T(4,128)(2,1)S(1)} %copy.685, bf16[3,48,1,258]{1,0,3,2:T(4,128)(2,1)S(1)} %maximum_select_fusion), kind=kLoop, calls=%fused_computation.249 | loop fusion | flops 5052672 | bytes 5052672 | tf_op jit(solution)/shard_map/concatenate | solution.py:112
  176.7 6.6 pad.60
  183.2 24.2 %copy.775 = bf16[48,34,3,8,33]{4,3,0,2,1:T(8,128)(2,1)} copy(bf16[48,34,3,8,33]{0,2,4,3,1:T(4,128)(2,1)} %bitcast.312) | data formatting | bytes 5170176 | tf_op jit(solution)/shard_map/conv_general_dilated | solution.py:34
  207.4 11.7 slice.977
  219.1 14.9 %fusion.14 = bf16[48,34,3,8,35]{4,3,0,2,1:T(8,128)(2,1)} fusion(bf16[48,34,3,7,2]{4,3,0,2,1:T(8,128)(2,1)} %slice.977, bf16[48,34,3,8,33]{4,3,0,2,1:T(8,128)(2,1)} %copy.775), kind=kLoop, calls=%fused_computation.31 | loop fusion | flops 8225280 | bytes 5463936 | tf_op jit(solution)/shard_map/conv_general_dilated | solution.py:34
  234.1 14.1 %copy.690 = bf16[48,34,3,8,35]{0,3,2,4,1:T(8,128)(2,1)} copy(bf16[48,34,3,8,35]{4,3,0,2,1:T(8,128)(2,1)} %fusion.14) | data formatting | bytes 5483520 | tf_op jit(solution)/shard_map/conv_general_dilated | solution.py:34
  248.2 23.5 %fusion.7 = (f32[32,24,33,48]{3,1,2,0:T(8,128)}, bf16[32,24,33,48]{3,1,2,0:T(8,128)(2,1)S(1)}) fusion(f32[48]{0:T(128)S(1)} %copy-done.51, pred[24,33]{0,1:T(8,128)(4,1)S(1)} %copy-done.55, bf16[48,48,3,3]{1,0,3,2:T(8,128)(2,1)S(1)} %copy-done.49, bf16[48,34,3,8,35]{0,3,2,4,1:T(8,128)(2,1)} %copy.690), kind=kOutput, calls=%fused_computation.16 | convolution fusion | flops 1065664512 | bytes 10083288 | tf_op jit(solution)/shard_map/conv_general_dilated | solution.py:34
  277.3 11.5 copy.842
  291.2 53.6 %all-gather.13.cloned.1.call-done = bf16[8,3,4,48,256]{4,3,2,1,0:T(8,128)(2,1)} async-done(((bf16[1,3,4,48,256]{4,3,2,1,0:T(8,128)(2,1)}), bf16[8,3,4,48,256]{4,3,2,1,0:T(8,128)(2,1)}) %all-gather.13.cloned.1.call-update) | async-done | bytes 2359312 | tf_op jit(solution)/shard_map/all_gather | solution.py:59
  348.2 57.5 %all-gather.15.cloned.1.call-done = bf16[3,4,48,1024]{2,1,0,3:T(4,128)(2,1)} async-done(((bf16[3,4,48,32]{2,1,0,3:T(4,128)(2,1)}), bf16[3,4,48,1024]{2,1,0,3:T(4,128)(2,1)}) %all-gather.15.cloned.1.call-update) | async-done | bytes 1179664 | tf_op jit(solution)/shard_map/all_gather | solution.py:71
  418.1 10.2 collective-permute-done.2
  428.9 19.1 %fusion.95 = bf16[48,34,3,258]{0,2,3,1:T(4,128)(2,1)S(1)} fusion(bf16[3,48,1,258]{1,0,3,2:T(4,128)(2,1)S(1)} %maximum_select_fusion.3, bf16[3,48,32,1]{1,0,3,2:T(4,128)(2,1)S(1)} %copy.708, bf16[3,48,32,256]{1,0,3,2:T(4,128)(2,1)} %bitcast.307, bf16[3,48,32,1]{1,0,3,2:T(4,128)(2,1)S(1)} %copy.707, bf16[3,48,1,258]{1,0,3,2:T(4,128)(2,1)S(1)} %maximum_select_fusion.2), kind=kLoop, calls=%fused_computation.246 | loop fusion | flops 5052672 | bytes 5052672 | tf_op jit(solution)/shard_map/concatenate | solution.py:112
  448.1 6.6 pad.62
  454.7 24.2 %copy.780 = bf16[48,34,3,8,33]{4,3,0,2,1:T(8,128)(2,1)} copy(bf16[48,34,3,8,33]{0,2,4,3,1:T(4,128)(2,1)} %bitcast.313) | data formatting | bytes 5170176 | tf_op jit(solution)/shard_map/conv_general_dilated | solution.py:34
  478.8 11.7 slice.997
  490.6 14.9 %fusion.15 = bf16[48,34,3,8,35]{4,3,0,2,1:T(8,128)(2,1)} fusion(bf16[48,34,3,7,2]{4,3,0,2,1:T(8,128)(2,1)} %slice.997, bf16[48,34,3,8,33]{4,3,0,2,1:T(8,128)(2,1)} %copy.780), kind=kLoop, calls=%fused_computation.32 | loop fusion | flops 8225280 | bytes 5463936 | tf_op jit(solution)/shard_map/conv_general_dilated | solution.py:34
  505.5 14.0 %copy.711 = bf16[48,34,3,8,35]{0,3,2,4,1:T(8,128)(2,1)} copy(bf16[48,34,3,8,35]{4,3,0,2,1:T(8,128)(2,1)} %fusion.15) | data formatting | bytes 5483520 | tf_op jit(solution)/shard_map/conv_general_dilated | solution.py:34
  519.5 22.3 %fusion.11 = (f32[32,24,33,48]{3,1,2,0:T(8,128)}, bf16[32,24,33,48]{3,1,2,0:T(8,128)(2,1)}) fusion(f32[48]{0:T(128)S(1)} %copy-done.52, pred[24,33]{0,1:T(8,128)(4,1)S(1)} %copy-done.55, bf16[48,48,3,3]{1,0,3,2:T(8,128)(2,1)S(1)} %copy-done, bf16[48,34,3,8,35]{0,3,2,4,1:T(8,128)(2,1)} %copy.711), kind=kOutput, calls=%fused_computation.20 | convolution fusion | flops 1065664512 | bytes 10083288 | tf_op jit(solution)/shard_map/conv_general_dilated | solution.py:34
  541.8 11.9 copy.713
  553.7 10.7 slice.999
  564.3 11.7 copy.800
  576.1 4.8 convert_reduce_fusion.1
  581.5 4.4 collective-permute-start.4
  590.6 4.4 collective-permute-done.4
  600.2 14.1 %reshape.2059 = bf16[48,34,3,8,33]{4,3,0,2,1:T(8,128)(2,1)} reshape(bf16[48,34,3,264]{3,0,2,1:T(8,128)(2,1)} %pad.64.clone) | data formatting | bytes 5170176 | tf_op jit(solution)/shard_map/conv_general_dilated | solution.py:34
  614.3 11.7 slice.1000
  626.0 14.9 %fusion.16 = bf16[48,34,3,8,35]{4,3,0,2,1:T(8,128)(2,1)} fusion(bf16[48,34,3,7,2]{4,3,0,2,1:T(8,128)(2,1)} %slice.1000, bf16[48,34,3,8,33]{4,3,0,2,1:T(8,128)(2,1)} %reshape.2059), kind=kLoop, calls=%fused_computation.33 | loop fusion | flops 8225280 | bytes 5463936 | tf_op jit(solution)/shard_map/conv_general_dilated | solution.py:34
  641.0 14.0 %copy.719 = bf16[48,34,3,8,35]{0,3,2,4,1:T(8,128)(2,1)} copy(bf16[48,34,3,8,35]{4,3,0,2,1:T(8,128)(2,1)} %fusion.16) | data formatting | bytes 5483520 | tf_op jit(solution)/shard_map/conv_general_dilated | solution.py:34
  655.0 22.2 %convolution_select_fusion.1 = f32[34,24,33,48]{3,1,2,0:T(8,128)} fusion(bf16[48,48,3,3]{1,0,3,2:T(8,128)(2,1)S(1)} %copy-done, bf16[48,34,3,8,35]{0,3,2,4,1:T(8,128)(2,1)} %copy.719, pred[24,33]{0,1:T(8,128)(4,1)S(1)} %copy-done.53), kind=kOutput, calls=%fused_computation.36 | convolution fusion | flops 1096153344 | bytes 7954200 | tf_op jit(solution)/shard_map/conv_general_dilated | solution.py:34
  677.2 13.6 %copy.720 = f32[34,24,33,48]{3,2,1,0:T(8,128)} copy(f32[34,24,33,48]{3,1,2,0:T(8,128)} %convolution_select_fusion.1) | data formatting | bytes 10340352 | tf_op jit(solution)/shard_map/conv_general_dilated | solution.py:34
  690.7 15.8 %reshape.2063 = f32[34,3,264,48]{3,2,1,0:T(8,128)} reshape(f32[34,24,33,48]{3,2,1,0:T(8,128)} %copy.720) | data formatting | bytes 10340352 | tf_op jit(solution)/shard_map/conv_general_dilated | solution.py:34
  706.6 10.7 slice_bitcast_fusion.1
  724.0 55.0 %all-gather.17.cloned.1.call-done = bf16[8,3,4,48,256]{4,3,2,1,0:T(8,128)(2,1)} async-done(((bf16[1,3,4,48,256]{4,3,2,1,0:T(8,128)(2,1)}), bf16[8,3,4,48,256]{4,3,2,1,0:T(8,128)(2,1)}) %all-gather.17.cloned.1.call-update) | async-done | bytes 2359312 | tf_op jit(solution)/shard_map/all_gather | solution.py:59
  782.0 12.0 copy.744
  793.9 10.6 slice.1027
  804.5 7.0 copy.766
  811.5 11.3 slice.1002
  822.9 17.1 %all-gather.19.cloned.1.call-done = bf16[3,4,48,1024]{2,1,0,3:T(4,128)(2,1)} async-done(((bf16[3,4,48,32]{2,1,0,3:T(4,128)(2,1)}), bf16[3,4,48,1024]{2,1,0,3:T(4,128)(2,1)}) %all-gather.19.cloned.1.call-update) | async-done | bytes 1179664 | tf_op jit(solution)/shard_map/all_gather | solution.py:71
  857.0 14.0 %convert_reduce_fusion = (f32[48]{0:T(128)}, bf16[3,48,32,256]{1,3,0,2:T(8,128)(2,1)S(1)}) fusion(f32[3,48,32,256]{1,3,0,2:T(8,128)} %scatter-add.99, f32[32,3,256,48]{3,0,2,1:T(8,128)} %slice.1027), kind=kLoop, calls=%fused_computation.30 | loop fusion | flops 4718544 | bytes 11796672 | tf_op jit(solution)/shard_map/reduce_sum | solution.py:215
  879.9 45.5 %fusion.87 = f32[48,48,3,3]{0,1,3,2:T(8,128)} fusion(bf16[3,48,32,256]{1,0,3,2:T(4,128)(2,1)} %copy.766, bf16[3,48,1,258]{1,0,3,2:T(4,128)(2,1)S(1)} %copy-done.17, bf16[3,48,32,1]{1,0,3,2:T(4,128)(2,1)S(1)} %copy-done.23, bf16[3,48,32,256]{1,0,3,2:T(4,128)(2,1)} %bitcast.308, bf16[3,48,32,1]{1,0,3,2:T(4,128)(2,1)S(1)} %copy-done.25, ...), kind=kOutput, calls=%fused_computation.245 | convolution fusion | flops 1031847552 | bytes 4968576 | tf_op jit(solution)/shard_map/conv_general_dilated | solution.py:172
  927.9 4.9 maximum_bitcast_fusion
  932.8 8.1 copy.819
  940.9 5.9 pad.66.clone
  946.8 14.1 %reshape.2066 = bf16[48,34,3,8,33]{4,3,0,2,1:T(8,128)(2,1)} reshape(bf16[48,34,3,264]{3,0,2,1:T(8,128)(2,1)} %pad.66.clone) | data formatting | bytes 5170176 | tf_op jit(solution)/shard_map/conv_general_dilated | solution.py:34
  960.9 11.7 slice.1028
  972.7 14.9 %fusion.17 = bf16[48,34,3,8,35]{4,3,0,2,1:T(8,128)(2,1)} fusion(bf16[48,34,3,7,2]{4,3,0,2,1:T(8,128)(2,1)} %slice.1028, bf16[48,34,3,8,33]{4,3,0,2,1:T(8,128)(2,1)} %reshape.2066), kind=kLoop, calls=%fused_computation.34 | loop fusion | flops 8225280 | bytes 5463936 | tf_op jit(solution)/shard_map/conv_general_dilated | solution.py:34
  987.6 14.1 %copy.747 = bf16[48,34,3,8,35]{0,3,2,4,1:T(8,128)(2,1)} copy(bf16[48,34,3,8,35]{4,3,0,2,1:T(8,128)(2,1)} %fusion.17) | data formatting | bytes 5483520 | tf_op jit(solution)/shard_map/conv_general_dilated | solution.py:34
  1001.7 22.0 %convolution_select_fusion = f32[34,24,33,48]{3,1,2,0:T(8,128)} fusion(bf16[48,48,3,3]{1,0,3,2:T(8,128)(2,1)S(1)} %copy-done.50, bf16[48,34,3,8,35]{0,3,2,4,1:T(8,128)(2,1)} %copy.747, pred[24,33]{0,1:T(8,128)(4,1)S(1)} %copy-done.54), kind=kOutput, calls=%fused_computation.35 | convolution fusion | flops 1096153344 | bytes 7954200 | tf_op jit(solution)/shard_map/conv_general_dilated | solution.py:34
  1023.7 13.4 copy.782
  1037.2 6.3 slice_bitcast_fusion
  1043.7 5.3 copy-done.5
  1054.1 48.8 %fusion.18 = f32[48,48,3,3]{0,1,3,2:T(8,128)} fusion(bf16[3,48,32,256]{1,3,0,2:T(8,128)(2,1)} %copy-done.3, bf16[3,48,1,258]{1,0,3,2:T(4,128)(2,1)S(1)} %copy-done.13, bf16[3,48,32,1]{1,0,3,2:T(4,128)(2,1)S(1)} %copy-done.19, bf16[3,48,32,256]{1,0,3,2:T(4,128)(2,1)} %copy.686, bf16[3,48,32,1]{1,0,3,2:T(4,128)(2,1)S(1)} %copy-done.21, ...), kind=kOutput, calls=%fused_computation.40 | convolution fusion | flops 1031847552 | bytes 4968576 | tf_op jit(solution)/shard_map/conv_general_dilated | solution.py:172
  1118.1 10.1 copy.767
  1128.2 39.3 %all-reduce.2 = (f32[48]{0:T(128)S(1)}, f32[48]{0:T(128)S(1)}) all-reduce(f32[48]{0:T(128)S(1)} %copy-done.48, f32[48]{0:T(128)S(1)} %copy-done.47), channel_id=1, replica_groups=mesh['face'=4,'tile'=8] {'face','tile'}, use_global_device_ids=true, to_apply=%region_6.7 | all-reduce | flops 96 | bytes 768 | tf_op jit(solution)/shard_map/psum | solution.py:219
  1168.0 12.0 slice.1030
  1180.0 16.4 %copy.814 = f32[3,48,32,256]{1,3,0,2:T(8,128)} copy(f32[3,48,32,256]{1,2,3,0:T(8,128)} %slice.1030) | data formatting | bytes 9437184
  1196.4 41.8 %all-reduce.6.cloned.1.call-done = (f32[48,48,3,3]{0,1,3,2:T(8,128)}, f32[48,48,3,3]{0,1,3,2:T(8,128)}) async-done(((f32[48,48,3,3]{0,1,3,2:T(8,128)}, f32[48,48,3,3]{0,1,3,2:T(8,128)}), (f32[48,48,3,3]{0,1,3,2:T(8,128)}, f32[48,48,3,3]{0,1,3,2:T(8,128)})) %all-reduce.6.cloned.1.call-update) | async-done | bytes 165904 | tf_op jit(solution)/shard_map/psum | solution.py:219
  1240.9 61.3 %all-gather.23.cloned.1.call-done = bf16[3,4,48,1024]{2,1,0,3:T(4,128)(2,1)} async-done(((bf16[3,4,48,32]{2,1,0,3:T(4,128)(2,1)}), bf16[3,4,48,1024]{2,1,0,3:T(4,128)(2,1)}) %all-gather.23.cloned.1.call-update) | async-done | bytes 1179664 | tf_op jit(solution)/shard_map/all_gather | solution.py:71
  1320.9 8.6 convert_element_type.355
  1329.5 7.2 copy.768
  (340 shorter events, 143.0 us)
Async XLA Ops:
  7.2 512.3 %copy-start = (bf16[48,48,3,3]{1,0,3,2:T(8,128)(2,1)S(1)}, bf16[48,48,3,3]{1,0,3,2:T(8,128)(2,1)}, u32[]{:S(2)}) copy-start(bf16[48,48,3,3]{1,0,3,2:T(8,128)(2,1)} %param.60) | copy-start | bytes 124420
  7.2 69.9 %copy-start.6 = (bf16[3,48,32,256]{3,2,1,0:T(8,128)(2,1)S(1)}, bf16[3,48,32,256]{3,2,1,0:T(8,128)(2,1)}, u32[]{:S(2)}) copy-start(bf16[3,48,32,256]{3,2,1,0:T(8,128)(2,1)} %param.56) | copy-start | bytes 7077892
  7.2 66.9 %all-gather.9.cloned.1.call-start = ((), (), s32[]{:S(2)}) async-start(), calls=%async_computation | async-start | bytes 2654208 | tf_op jit(solution)/shard_map/all_gather | solution.py:59
  12.5 71.4 %copy-start.26 = (s32[12,4,3]{0,1,2:T(4,128)S(1)}, s32[12,4,3]{0,1,2:T(4,128)}, u32[]{:S(2)}) copy-start(s32[12,4,3]{0,1,2:T(4,128)} %param.62) | copy-start | bytes 1732
  12.5 71.9 %copy-start.46 = (s32[12,4]{0,1:T(4,128)S(1)}, s32[12,4]{0,1:T(4,128)}, u32[]{:S(2)}) copy-start(s32[12,4]{0,1:T(4,128)} %param.63) | copy-start | bytes 580
  18.3 116.9 %all-gather.11.cloned.1.call-start = ((), (), s32[]{:S(2)}) async-start(), calls=%async_computation.1 | async-start | bytes 3244032 | tf_op jit(solution)/shard_map/all_gather | solution.py:71
  77.0 267.7 %all-gather.13.cloned.1.call-start = ((), (), s32[]{:S(2)}) async-start(), calls=%async_computation.2 | async-start | bytes 2654208 | tf_op jit(solution)/shard_map/all_gather | solution.py:59
  84.2 325.4 %copy-start.27 = (pred[12]{0:T(512)(128)(4,1)}, pred[12]{0:T(512)(128)(4,1)S(1)}, u32[]{:S(2)}) copy-start(pred[12]{0:T(512)(128)(4,1)S(1)} %eq.133) | copy-start | bytes 40
  85.4 320.3 %copy-start.7 = (s32[12]{0:T(128)}, s32[12]{0:T(128)S(1)}, u32[]{:S(2)}) copy-start(s32[12]{0:T(128)S(1)} %fusion.73) | copy-start | bytes 148
  140.6 36.0 %copy-start.18 = (bf16[3,48,32,1]{1,0,3,2:T(4,128)(2,1)}, bf16[3,48,32,1]{1,0,3,2:T(4,128)(2,1)S(1)}, u32[]{:S(2)}) copy-start(bf16[3,48,32,1]{1,0,3,2:T(4,128)(2,1)S(1)} %copy.687) | copy-start | bytes 27652
  140.8 35.8 %copy-start.20 = (bf16[3,48,32,1]{1,0,3,2:T(4,128)(2,1)}, bf16[3,48,32,1]{1,0,3,2:T(4,128)(2,1)S(1)}, u32[]{:S(2)}) copy-start(bf16[3,48,32,1]{1,0,3,2:T(4,128)(2,1)S(1)} %copy.685) | copy-start | bytes 27652
  141.3 17.5 %copy-start.2 = (bf16[3,48,32,256]{1,0,3,2:T(4,128)(2,1)S(1)}, bf16[3,48,32,256]{1,0,3,2:T(4,128)(2,1)}, u32[]{:S(2)}) copy-start(bf16[3,48,32,256]{1,0,3,2:T(4,128)(2,1)} %copy.686) | copy-start | bytes 7077892
  143.0 15.3 %collective-permute-start = (bf16[3,48,1,258]{1,0,3,2:T(4,128)(2,1)S(1)}, bf16[3,48,1,258]{1,0,3,2:T(4,128)(2,1)S(1)}, u32[]{:S(2)}, u32[]{:S(2)}) collective-permute-start(bf16[3,48,1,258]{1,0,3,2:T(4,128)(2,1)S(1)} %get-tuple-element.393), channel_id=1, source_target_pairs={{0,1},{1,2},{2,3},{3,4},{4,5},{5,6},{6,7},{8,9},{9,10},{10,11},{11... | collective-permute-start | bytes 222920 | tf_op jit(solution)/shard_map/ppermute | solution.py:19
  146.6 11.9 collective-permute-start.1
  158.5 24.7 %copy-start.10 = (bf16[3,48,1,258]{1,0,3,2:T(4,128)(2,1)}, bf16[3,48,1,258]{1,0,3,2:T(4,128)(2,1)S(1)}, u32[]{:S(2)}) copy-start(bf16[3,48,1,258]{1,0,3,2:T(4,128)(2,1)S(1)} %maximum_select_fusion) | copy-start | bytes 222916
  158.8 24.4 %copy-start.12 = (bf16[3,48,1,258]{1,0,3,2:T(4,128)(2,1)}, bf16[3,48,1,258]{1,0,3,2:T(4,128)(2,1)S(1)}, u32[]{:S(2)}) copy-start(bf16[3,48,1,258]{1,0,3,2:T(4,128)(2,1)S(1)} %maximum_select_fusion.1) | copy-start | bytes 222916
  234.1 14.1 %copy-start.49 = (bf16[48,48,3,3]{1,0,3,2:T(8,128)(2,1)S(1)}, bf16[48,48,3,3]{1,0,3,2:T(8,128)(2,1)}, u32[]{:S(2)}) copy-start(bf16[48,48,3,3]{1,0,3,2:T(8,128)(2,1)} %param.58) | copy-start | bytes 124420
  234.1 14.1 %copy-start.51 = (f32[48]{0:T(128)S(1)}, f32[48]{0:T(128)}, u32[]{:S(2)}) copy-start(f32[48]{0:T(128)} %param.59) | copy-start | bytes 580
  234.1 14.1 %copy-start.55 = (pred[24,33]{0,1:T(8,128)(4,1)S(1)}, pred[24,33]{0,1:T(8,128)(4,1)}, u32[]{:S(2)}) copy-start(pred[24,33]{0,1:T(8,128)(4,1)} %constant.719) | copy-start | bytes 2380
  291.1 114.6 %all-gather.15.cloned.1.call-start = ((), (), s32[]{:S(2)}) async-start(), calls=%async_computation.3 | async-start | bytes 3244032 | tf_op jit(solution)/shard_map/all_gather | solution.py:71
  347.7 431.3 %all-gather.17.cloned.1.call-start = ((), (), s32[]{:S(2)}) async-start(), calls=%async_computation.4 | async-start | bytes 2654208 | tf_op jit(solution)/shard_map/all_gather | solution.py:59
  411.2 36.9 %copy-start.22 = (bf16[3,48,32,1]{1,0,3,2:T(4,128)(2,1)}, bf16[3,48,32,1]{1,0,3,2:T(4,128)(2,1)S(1)}, u32[]{:S(2)}) copy-start(bf16[3,48,32,1]{1,0,3,2:T(4,128)(2,1)S(1)} %copy.708) | copy-start | bytes 27652
  411.4 36.7 %copy-start.24 = (bf16[3,48,32,1]{1,0,3,2:T(4,128)(2,1)}, bf16[3,48,32,1]{1,0,3,2:T(4,128)(2,1)S(1)}, u32[]{:S(2)}) copy-start(bf16[3,48,32,1]{1,0,3,2:T(4,128)(2,1)S(1)} %copy.707) | copy-start | bytes 27652
  413.3 15.0 %collective-permute-start.2 = (bf16[3,48,1,258]{1,0,3,2:T(4,128)(2,1)S(1)}, bf16[3,48,1,258]{1,0,3,2:T(4,128)(2,1)S(1)}, u32[]{:S(2)}, u32[]{:S(2)}) collective-permute-start(bf16[3,48,1,258]{1,0,3,2:T(4,128)(2,1)S(1)} %get-tuple-element.391), channel_id=1, source_target_pairs={{0,1},{1,2},{2,3},{3,4},{4,5},{5,6},{6,7},{8,9},{9,10},{10,11},{11... | collective-permute-start | bytes 222920 | tf_op jit(solution)/shard_map/ppermute | solution.py:19
  416.7 11.9 collective-permute-start.3
  428.6 26.0 %copy-start.14 = (bf16[3,48,1,258]{1,0,3,2:T(4,128)(2,1)}, bf16[3,48,1,258]{1,0,3,2:T(4,128)(2,1)S(1)}, u32[]{:S(2)}) copy-start(bf16[3,48,1,258]{1,0,3,2:T(4,128)(2,1)S(1)} %maximum_select_fusion.2) | copy-start | bytes 222916
  428.9 25.7 %copy-start.16 = (bf16[3,48,1,258]{1,0,3,2:T(4,128)(2,1)}, bf16[3,48,1,258]{1,0,3,2:T(4,128)(2,1)S(1)}, u32[]{:S(2)}) copy-start(bf16[3,48,1,258]{1,0,3,2:T(4,128)(2,1)S(1)} %maximum_select_fusion.3) | copy-start | bytes 222916
  505.5 14.0 %copy-start.52 = (f32[48]{0:T(128)S(1)}, f32[48]{0:T(128)}, u32[]{:S(2)}) copy-start(f32[48]{0:T(128)} %param.61) | copy-start | bytes 580
  581.5 13.4 collective-permute-start.4
  586.0 9.0 collective-permute-start.5
  587.6 132.2 %copy-start.34 = (pred[3]{0:T(512)(128)(4,1)}, pred[3]{0:T(512)(128)(4,1)S(1)}, u32[]{:S(2)}) copy-start(pred[3]{0:T(512)(128)(4,1)S(1)} %get-tuple-element.343) | copy-start | bytes 13
  587.6 132.2 %copy-start.40 = (pred[3]{0:T(512)(128)(4,1)}, pred[3]{0:T(512)(128)(4,1)S(1)}, u32[]{:S(2)}) copy-start(pred[3]{0:T(512)(128)(4,1)S(1)} %get-tuple-element.344) | copy-start | bytes 13
  587.6 132.2 %copy-start.42 = (pred[3]{0:T(512)(128)(4,1)}, pred[3]{0:T(512)(128)(4,1)S(1)}, u32[]{:S(2)}) copy-start(pred[3]{0:T(512)(128)(4,1)S(1)} %get-tuple-element.348) | copy-start | bytes 13
  587.6 132.2 %copy-start.44 = (pred[3]{0:T(512)(128)(4,1)}, pred[3]{0:T(512)(128)(4,1)S(1)}, u32[]{:S(2)}) copy-start(pred[3]{0:T(512)(128)(4,1)S(1)} %get-tuple-element.349) | copy-start | bytes 13
  587.6 133.3 %copy-start.30 = (pred[3]{0:T(512)(128)(4,1)}, pred[3]{0:T(512)(128)(4,1)S(1)}, u32[]{:S(2)}) copy-start(pred[3]{0:T(512)(128)(4,1)S(1)} %get-tuple-element.345) | copy-start | bytes 13
  587.6 133.3 %copy-start.32 = (pred[3]{0:T(512)(128)(4,1)}, pred[3]{0:T(512)(128)(4,1)S(1)}, u32[]{:S(2)}) copy-start(pred[3]{0:T(512)(128)(4,1)S(1)} %get-tuple-element.342) | copy-start | bytes 13
  587.6 133.3 %copy-start.36 = (pred[3]{0:T(512)(128)(4,1)}, pred[3]{0:T(512)(128)(4,1)S(1)}, u32[]{:S(2)}) copy-start(pred[3]{0:T(512)(128)(4,1)S(1)} %get-tuple-element.346) | copy-start | bytes 13
  587.6 133.3 %copy-start.38 = (pred[3]{0:T(512)(128)(4,1)}, pred[3]{0:T(512)(128)(4,1)S(1)}, u32[]{:S(2)}) copy-start(pred[3]{0:T(512)(128)(4,1)S(1)} %get-tuple-element.347) | copy-start | bytes 13
  641.0 14.0 %copy-start.53 = (pred[24,33]{0,1:T(8,128)(4,1)S(1)}, pred[24,33]{0,1:T(8,128)(4,1)}, u32[]{:S(2)}) copy-start(pred[24,33]{0,1:T(8,128)(4,1)} %constant.721) | copy-start | bytes 2380
  723.9 116.1 %all-gather.19.cloned.1.call-start = ((), (), s32[]{:S(2)}) async-start(), calls=%async_computation.5 | async-start | bytes 3244032 | tf_op jit(solution)/shard_map/all_gather | solution.py:71
  781.9 325.5 %all-gather.21.cloned.1.call-start = ((), (), s32[]{:S(2)}) async-start(), calls=%async_computation.6 | async-start | bytes 2654208 | tf_op jit(solution)/shard_map/all_gather | solution.py:59
  811.5 28.5 %copy-start.8 = (s32[12]{0:T(128)S(1)}, s32[12]{0:T(128)}, u32[]{:S(2)}) copy-start(s32[12]{0:T(128)} %copy-done.7) | copy-start | bytes 148
  811.5 32.3 %copy-start.28 = (pred[12]{0:T(512)(128)(4,1)S(1)}, pred[12]{0:T(512)(128)(4,1)}, u32[]{:S(2)}) copy-start(pred[12]{0:T(512)(128)(4,1)} %copy-done.27) | copy-start | bytes 40
  857.0 22.9 %copy-start.15 = (bf16[3,48,1,258]{1,0,3,2:T(4,128)(2,1)S(1)}, bf16[3,48,1,258]{1,0,3,2:T(4,128)(2,1)}, u32[]{:S(2)}) copy-start(bf16[3,48,1,258]{1,0,3,2:T(4,128)(2,1)} %copy-done.14) | copy-start | bytes 222916
  857.0 23.0 %copy-start.17 = (bf16[3,48,1,258]{1,0,3,2:T(4,128)(2,1)S(1)}, bf16[3,48,1,258]{1,0,3,2:T(4,128)(2,1)}, u32[]{:S(2)}) copy-start(bf16[3,48,1,258]{1,0,3,2:T(4,128)(2,1)} %copy-done.16) | copy-start | bytes 222916
  857.0 23.0 %copy-start.23 = (bf16[3,48,32,1]{1,0,3,2:T(4,128)(2,1)S(1)}, bf16[3,48,32,1]{1,0,3,2:T(4,128)(2,1)}, u32[]{:S(2)}) copy-start(bf16[3,48,32,1]{1,0,3,2:T(4,128)(2,1)} %copy-done.22) | copy-start | bytes 27652
  857.0 23.0 %copy-start.25 = (bf16[3,48,32,1]{1,0,3,2:T(4,128)(2,1)S(1)}, bf16[3,48,32,1]{1,0,3,2:T(4,128)(2,1)}, u32[]{:S(2)}) copy-start(bf16[3,48,32,1]{1,0,3,2:T(4,128)(2,1)} %copy-done.24) | copy-start | bytes 27652
  874.6 53.3 %collective-permute-start.6 = (bf16[3,48,1,258]{1,3,0,2:T(8,128)(2,1)}, bf16[3,48,1,258]{1,3,0,2:T(8,128)(2,1)}, u32[]{:S(2)}, u32[]{:S(2)}) collective-permute-start(bf16[3,48,1,258]{1,3,0,2:T(8,128)(2,1)} %get-tuple-element.397), channel_id=1, source_target_pairs={{0,1},{1,2},{2,3},{3,4},{4,5},{5,6},{6,7},{8,9},{9,10},{10,11},{11... | collective-permute-start | bytes 222920 | tf_op jit(solution)/shard_map/ppermute | solution.py:19
  878.6 49.3 %collective-permute-start.7 = (bf16[3,48,1,258]{1,3,0,2:T(8,128)(2,1)}, bf16[3,48,1,258]{1,3,0,2:T(8,128)(2,1)}, u32[]{:S(2)}, u32[]{:S(2)}) collective-permute-start(bf16[3,48,1,258]{1,3,0,2:T(8,128)(2,1)} %get-tuple-element.398), channel_id=1, source_target_pairs={{1,0},{2,1},{3,2},{4,3},{5,4},{6,5},{7,6},{9,8},{10,9},{11,10},{12... | collective-permute-start | bytes 222920 | tf_op jit(solution)/shard_map/ppermute | solution.py:22
  879.9 45.5 %copy-start.4 = (bf16[3,48,32,256]{1,3,0,2:T(8,128)(2,1)S(1)}, bf16[3,48,32,256]{1,3,0,2:T(8,128)(2,1)}, u32[]{:S(2)}) copy-start(bf16[3,48,32,256]{1,3,0,2:T(8,128)(2,1)} %copy-done.3) | copy-start | bytes 7077892
  987.6 14.1 %copy-start.50 = (bf16[48,48,3,3]{1,0,3,2:T(8,128)(2,1)S(1)}, bf16[48,48,3,3]{1,0,3,2:T(8,128)(2,1)}, u32[]{:S(2)}) copy-start(bf16[48,48,3,3]{1,0,3,2:T(8,128)(2,1)} %param.58) | copy-start | bytes 124420
  987.6 14.1 %copy-start.54 = (pred[24,33]{0,1:T(8,128)(4,1)S(1)}, pred[24,33]{0,1:T(8,128)(4,1)}, u32[]{:S(2)}) copy-start(pred[24,33]{0,1:T(8,128)(4,1)} %constant.721) | copy-start | bytes 2380
  1037.2 14.5 %copy-start.31 = (pred[3]{0:T(512)(128)(4,1)S(1)}, pred[3]{0:T(512)(128)(4,1)}, u32[]{:S(2)}) copy-start(pred[3]{0:T(512)(128)(4,1)} %copy-done.30) | copy-start | bytes 13
  1037.2 16.9 %copy-start.11 = (bf16[3,48,1,258]{1,0,3,2:T(4,128)(2,1)S(1)}, bf16[3,48,1,258]{1,0,3,2:T(4,128)(2,1)}, u32[]{:S(2)}) copy-start(bf16[3,48,1,258]{1,0,3,2:T(4,128)(2,1)} %copy-done.10) | copy-start | bytes 222916
  1037.2 16.9 %copy-start.13 = (bf16[3,48,1,258]{1,0,3,2:T(4,128)(2,1)S(1)}, bf16[3,48,1,258]{1,0,3,2:T(4,128)(2,1)}, u32[]{:S(2)}) copy-start(bf16[3,48,1,258]{1,0,3,2:T(4,128)(2,1)} %copy-done.12) | copy-start | bytes 222916
  1037.2 16.9 %copy-start.19 = (bf16[3,48,32,1]{1,0,3,2:T(4,128)(2,1)S(1)}, bf16[3,48,32,1]{1,0,3,2:T(4,128)(2,1)}, u32[]{:S(2)}) copy-start(bf16[3,48,32,1]{1,0,3,2:T(4,128)(2,1)} %copy-done.18) | copy-start | bytes 27652
  1037.2 16.9 %copy-start.21 = (bf16[3,48,32,1]{1,0,3,2:T(4,128)(2,1)S(1)}, bf16[3,48,32,1]{1,0,3,2:T(4,128)(2,1)}, u32[]{:S(2)}) copy-start(bf16[3,48,32,1]{1,0,3,2:T(4,128)(2,1)} %copy-done.20) | copy-start | bytes 27652
  1054.0 184.1 %all-reduce.6.cloned.1.call-start = ((), (), s32[]{:S(2)}) async-start(), calls=%async_computation.8 | async-start | bytes 884736 | tf_op jit(solution)/shard_map/psum | solution.py:219
  1102.9 199.3 %all-gather.23.cloned.1.call-start = ((), (), s32[]{:S(2)}) async-start(), calls=%async_computation.7 | async-start | bytes 3244032 | tf_op jit(solution)/shard_map/all_gather | solution.py:71
  1114.3 13.9 %copy-start.47 = (f32[48]{0:T(128)S(1)}, f32[48]{0:T(128)}, u32[]{:S(2)}) copy-start(f32[48]{0:T(128)} %get-tuple-element.358) | copy-start | bytes 580
  1114.4 13.9 %copy-start.48 = (f32[48]{0:T(128)S(1)}, f32[48]{0:T(128)}, u32[]{:S(2)}) copy-start(f32[48]{0:T(128)} %get-tuple-element.360) | copy-start | bytes 580
  1180.0 122.2 %copy-start.9 = (s32[12]{0:T(128)S(1)}, s32[12]{0:T(128)}, u32[]{:S(2)}) copy-start(s32[12]{0:T(128)} %copy-done.7) | copy-start | bytes 148
  1180.0 126.2 %copy-start.29 = (pred[12]{0:T(512)(128)(4,1)S(1)}, pred[12]{0:T(512)(128)(4,1)}, u32[]{:S(2)}) copy-start(pred[12]{0:T(512)(128)(4,1)} %copy-done.27) | copy-start | bytes 40
  1318.1 18.6 %copy-start.1 = (bf16[48,48,3,3]{1,0,3,2:T(8,128)(2,1)S(1)}, bf16[48,48,3,3]{1,0,3,2:T(8,128)(2,1)}, u32[]{:S(2)}) copy-start(bf16[48,48,3,3]{1,0,3,2:T(8,128)(2,1)} %param.60) | copy-start | bytes 124420
  (9 other events, 79.6 us)
Sparse Core Ops, SparseCore 0:
  18.4 55.6 all-gather.8
  77.6 57.6 all-gather.10
  291.2 53.4 all-gather.12
  348.1 57.6 all-gather.14
  724.0 54.9 all-gather.16
  782.3 57.6 all-gather.18
  1054.2 53.1 all-gather.20
  1113.3 124.8 all-reduce.5
  1242.1 60.0 all-gather.22
